TPU v7x, 128 devices: a whole 4x4x4 slice. The times are simulated.
128 devices in a mesh: seq: 32 (over z, y, core), tp: 4 (over x).
Axes of the slice: x: 4, y: 4, z: 4, core: 2. Of those that a mesh axis runs over, the one named last changes fastest.
Arguments:
- tokens: bfloat16 [32768, 2048], P('seq', 'tp'), may hold values from -8 to 8
- col_order: int32 [32768], P('seq'), may hold values from 0 to 32767, as said below
- in_gain: float32 [2, 2048], replicated, may hold values from 0.5 to 1.5
- w_in: bfloat16 [2, 2048, 2, 2048], P(None, None, None, 'tp'), may hold values from -0.125 to 0.125
- w_bc: bfloat16 [2, 2048, 256], replicated, may hold values from -0.0625 to 0.0625
- w_dt: bfloat16 [2, 2048, 32], P(None, None, 'tp'), may hold values from -2 to 2
- conv_x: float32 [2, 4, 2048], P(None, None, 'tp'), may hold values from -3 to 3
- conv_bc: float32 [2, 4, 256], replicated, may hold values from -3 to 3
- dt_bias: float32 [2, 32], P(None, 'tp'), may hold values from -1 to 0.5
- a_log: float32 [2, 32], P(None, 'tp'), may hold values from -16 to -2, as said below
- d_skip: float32 [2, 32], P(None, 'tp'), may hold values from 0.5 to 2
- out_gain: float32 [2, 2048], P(None, 'tp'), may hold values from 0.5 to 1.5
- w_out: bfloat16 [2, 2048, 2048], P(None, 'tp'), may hold values from -0.125 to 0.125
Outputs:
- mixed_out: bfloat16 [32768, 2048], P('seq', 'tp')
Inputs may be any that keep to these rules, and one draw needn't show every extreme that they name: `col_order`: A permutation of the 32768 positions of a frame of 64 rows and 512 columns stored row by row: the column order visits the columns one after another in a drawn order, each from top to bottom or from bottom to top as drawn. So every aligned block of 1024 positions takes exactly 32 row-order positions from each aligned block of 1024 row-order positions. Each head's decay rate exp(a_log) is either between about one in fifty and one in seventeen a step or between 0.3 / 32768 and 2 / 32768 a step.
All inputs are finite; a program needn't handle non-finite values.
Results may differ from a plain program's by a relative error of at most 0.024.
Values may be sent and summed in bfloat16 or wider, within the bound.
No kernel may reach another device: no remote copies, remote signals or barrier semaphores. Data moves between devices by JAX's collectives and lax.ppermute only.
A program may use at most 128 MiB of HBM per device.

v0:
```python
import jax
import jax.numpy as jnp
from jax import lax
from jax.sharding import Mesh
from jax.sharding import PartitionSpec as P

HEAD_DIM = 64
STATE = 128
STRETCH = 128
SEQ = ("seq_0", "seq_1", "seq_2")
highest = lax.Precision.HIGHEST
epsilon = 1e-05


def laid_out(blocks, dim):
    blocks = jnp.moveaxis(blocks, 0, dim)
    lengths = blocks.shape
    return blocks.reshape(*lengths[:dim], lengths[dim] * lengths[dim + 1], *lengths[dim + 2 :])


def sent_to_all(x, axis):
    devices = lax.axis_size(axis)
    return lax.all_to_all(jnp.broadcast_to(x[None], (devices, *x.shape)), axis, 0, 0, tiled=True)


def gathered_copies(x, axis, dim):
    return laid_out(sent_to_all(x, axis), dim)


def passed_along(x, axis, by):
    devices = lax.axis_size(axis)
    pairs = [(i, i + by) for i in range(devices) if 0 <= i + by < devices]
    return lax.ppermute(x, axis, pairs)


def in_blocks(x, dim, devices):
    lengths = x.shape
    blocks = x.reshape(*lengths[:dim], devices, lengths[dim] // devices, *lengths[dim + 1 :])
    return jnp.moveaxis(blocks, dim, 0)


def moved_by_axis(blocks, axes, turns):
    lengths = [lax.axis_size(a) for a in axes]
    blocks = blocks.reshape(*lengths, *blocks.shape[1:])
    for k in turns:
        blocks = lax.all_to_all(blocks, axes[k], split_axis=k, concat_axis=k, tiled=True)
    return blocks.reshape(-1, *blocks.shape[len(axes) :])


def exchange_by_chip(x, groups, turns, split_dim, concat_dim):
    devices = lax.axis_size(groups[0]) * lax.axis_size(groups[1])
    blocks = in_blocks(x, split_dim, devices)
    return laid_out(moved_by_axis(blocks, groups, turns), concat_dim)


def causal_mix(current, rim, taps):
    length = current.shape[0]
    extended = jnp.concatenate([rim, current], axis=0).astype(jnp.float32)
    mixed = jnp.zeros(current.shape, jnp.float32)
    for offset in range(taps.shape[0]):
        mixed = mixed + taps[offset] * extended[offset : offset + length]
    return mixed


def advance(state, pieces):
    factor, fresh = pieces
    return (factor[:, None, None] * state + fresh, state)


def incoming_state(local_end, device_log):
    count = lax.axis_size(SEQ)
    own_index = lax.axis_index(SEQ)
    gathered = gathered_copies(device_log, SEQ, 0).reshape(count, device_log.shape[0])
    before = jnp.cumsum(gathered, axis=0) - gathered
    earlier = (jnp.arange(count) < own_index)[:, None]
    own_prefix = jnp.sum(jnp.where(earlier, gathered, 0.0), axis=0)
    spans = jnp.where(earlier, own_prefix[None, :] - before - gathered, -jnp.inf)
    factors = jnp.exp(spans)
    return jnp.zeros(local_end.shape, jnp.float32) + jnp.einsum(
        "mh,mhpn->hpn",
        factors,
        lax.all_gather(local_end[None].astype(jnp.bfloat16), SEQ, axis=0, tiled=True).astype(
            jnp.float32
        ),
        precision=highest,
    )


def mixer(full, which, params):
    in_gain, w_in, w_bc, w_dt, conv_x, conv_bc, dt_bias, a_log, d_skip, out_gain, w_out = params
    row_count, model_width = full.shape
    inner = w_in.shape[3]
    head_count = inner // HEAD_DIM
    lag = conv_x.shape[1] - 1
    widen = full.astype(jnp.float32)
    scale = lax.rsqrt(jnp.mean(widen * widen, axis=-1, keepdims=True) + epsilon)
    normed = (widen * scale * in_gain[which]).astype(jnp.bfloat16)
    projected = jnp.dot(
        normed, w_in[which].reshape(model_width, 2 * inner), preferred_element_type=jnp.float32
    )
    pre_x = projected[:, :inner].astype(jnp.bfloat16)
    gate_z = projected[:, inner:].astype(jnp.bfloat16)
    pre_bc = jnp.dot(normed, w_bc[which], preferred_element_type=jnp.float32).astype(jnp.bfloat16)
    dt_raw = jnp.dot(normed, w_dt[which], preferred_element_type=jnp.float32)
    rim_x, rim_bc = passed_along((pre_x[row_count - lag :], pre_bc[row_count - lag :]), SEQ, 1)
    conv_out = jax.nn.silu(causal_mix(pre_x, rim_x, conv_x[which]))
    bc_out = jax.nn.silu(causal_mix(pre_bc, rim_bc, conv_bc[which]))
    step_size = jax.nn.softplus(dt_raw + dt_bias[which])
    decay_log = -step_size * jnp.exp(a_log[which])
    heads_in = conv_out.reshape(row_count, head_count, HEAD_DIM)
    feed = heads_in * step_size[:, :, None]
    blocks = row_count // STRETCH
    log_blocks = decay_log.reshape(blocks, STRETCH, head_count)
    b_blocks = bc_out[:, :STATE].reshape(blocks, STRETCH, STATE)
    c_blocks = bc_out[:, STATE:].reshape(blocks, STRETCH, STATE)
    feed_blocks = feed.reshape(blocks, STRETCH, head_count, HEAD_DIM)
    cumul = jnp.cumsum(log_blocks, axis=1)
    cumul_t = jnp.transpose(cumul, (0, 2, 1))
    lower = jnp.arange(STRETCH)[:, None] >= jnp.arange(STRETCH)[None, :]
    spread = jnp.where(lower[None, None], cumul_t[..., :, None] - cumul_t[..., None, :], -jnp.inf)
    intersection = jnp.einsum("cqn,ckn->cqk", c_blocks, b_blocks, precision=highest)
    inside = jnp.einsum(
        "chqk,ckhp->cqhp", intersection[:, None] * jnp.exp(spread), feed_blocks, precision=highest
    )
    to_end = jnp.exp(cumul_t[..., -1:] - cumul_t)
    fresh = jnp.einsum("chk,ckn,ckhp->chpn", to_end, b_blocks, feed_blocks, precision=highest)
    block_decay = jnp.exp(cumul_t[..., -1])
    start_state = jnp.zeros((head_count, HEAD_DIM, STATE), jnp.float32)
    local_end, entering = lax.scan(advance, start_state, (block_decay, fresh))
    carried = (
        jnp.einsum("cqn,chpn->cqhp", c_blocks, entering, precision=highest)
        * jnp.exp(cumul)[..., None]
    )
    block_sums = cumul[:, -1, :]
    prior = jnp.cumsum(block_sums, axis=0) - block_sums
    device_cumul = cumul + prior[:, None, :]
    device_log = jnp.sum(block_sums, axis=0)
    arriving = incoming_state(local_end, device_log)
    correction = (
        jnp.einsum("cqn,hpn->cqhp", c_blocks, arriving, precision=highest)
        * jnp.exp(device_cumul)[..., None]
    )
    ssd = (inside + carried + correction).reshape(row_count, head_count, HEAD_DIM) + d_skip[which][
        None, :, None
    ] * heads_in
    gated = ssd * jax.nn.silu(gate_z.astype(jnp.float32).reshape(row_count, head_count, HEAD_DIM))
    norm_scale = lax.rsqrt(jnp.mean(gated * gated, axis=-1, keepdims=True) + epsilon)
    mixed_heads = (
        (gated * norm_scale * out_gain[which].reshape(head_count, HEAD_DIM))
        .reshape(row_count, inner)
        .astype(jnp.bfloat16)
    )
    return jnp.dot(mixed_heads, w_out[which], preferred_element_type=jnp.float32)


def spread_features(piece):
    return lax.all_gather(piece, "tp", axis=1, tiled=True)


def collect_heads(partial_sum):
    return lax.psum_scatter(
        partial_sum.astype(jnp.bfloat16), "tp", scatter_dimension=1, tiled=True
    ).astype(jnp.float32)


def reorder_rows(stream, col_order):
    count = lax.axis_size(SEQ)
    row_count = stream.shape[0]
    block_rows = row_count // count
    source = col_order // row_count
    local_index = col_order % row_count
    grouping = jnp.argsort(source, stable=True)
    wanted = local_index[grouping].reshape(count, block_rows)
    asked = exchange_by_chip(wanted, (("seq_0", "seq_1"), "seq_2"), (1, 0), 0, 0)
    payload = stream[asked.reshape(-1)].reshape(count, block_rows, stream.shape[1])
    arrived = exchange_by_chip(payload, (("seq_0", "seq_1"), "seq_2"), (1, 0), 0, 0).reshape(
        row_count, stream.shape[1]
    )
    placement = jnp.argsort(grouping)
    return arrived[placement]


def body(
    tokens,
    col_order,
    in_gain,
    w_in,
    w_bc,
    w_dt,
    conv_x,
    conv_bc,
    dt_bias,
    a_log,
    d_skip,
    out_gain,
    w_out,
):
    params = (in_gain, w_in, w_bc, w_dt, conv_x, conv_bc, dt_bias, a_log, d_skip, out_gain, w_out)
    first_full = spread_features(tokens)
    first_part = mixer(first_full, 0, params)
    row_result = (tokens.astype(jnp.float32) + collect_heads(first_part)).astype(jnp.bfloat16)
    own_rows = reorder_rows(row_result, col_order)
    second_full = spread_features(own_rows)
    second_part = mixer(second_full, 1, params)
    return (own_rows.astype(jnp.float32) + collect_heads(second_part)).astype(jnp.bfloat16)


def solution(mesh):
    torus = Mesh(mesh.devices.reshape(4, 4, 2, mesh.shape["tp"]), ("seq_0", "seq_1", "seq_2", "tp"))
    return jax.shard_map(
        body,
        mesh=torus,
        in_specs=(
            P(SEQ, "tp"),
            P(SEQ),
            P(),
            P(None, None, None, "tp"),
            P(),
            P(None, None, "tp"),
            P(None, None, "tp"),
            P(),
            P(None, "tp"),
            P(None, "tp"),
            P(None, "tp"),
            P(None, "tp"),
            P(None, "tp", None),
        ),
        out_specs=P(SEQ, "tp"),
        check_vma=False,
    )
```

profile of v0, /device:TPU:1, one launch (start us, length us, event | category | flops | bytes accessed | tf_op | source)
XLA Modules:
  0.0 575.8 jit_solution(12658820675319592210)
XLA Ops:
  7.3 7.9 %fusion.98 = (bf16[1,2048,2,512]{3,2,1,0:T(2,128)(2,1)}, bf16[1,2048,2,512]{3,2,1,0:T(2,128)(2,1)S(1)}) fusion(bf16[2,2048,2,512]{3,2,1,0:T(2,128)(2,1)} %param.20), kind=kLoop, calls=%fused_computation.187 | loop fusion | bytes 16777216 | tf_op jit(solution)/shard_map/slice | solution.py:99
  15.3 3.2 copy.200
  20.9 39.6 %all-gather.8.cloned.1.call-done = bf16[1024,2048]{1,0:T(8,128)(2,1)} async-done(((bf16[1024,512]{1,0:T(8,128)(2,1)}), bf16[1024,2048]{1,0:T(8,128)(2,1)}) %all-gather.8.cloned.1.call-update) | async-done | bytes 4194320 | tf_op jit(solution)/shard_map/all_gather | solution.py:157
  60.5 3.2 fusion.2
  63.9 7.2 %convolution_convert_fusion.3 = bf16[1024,1024]{1,0:T(8,128)(2,1)S(1)} fusion(bf16[2048,1024]{1,0:T(8,128)(2,1)} %bitcast.229, bf16[1024,2048]{1,0:T(8,128)(2,1)S(1)} %copy-done.14, f32[2048]{0:T(1024)S(1)} %bitcast.255, f32[1024]{0:T(1024)S(1)} %add_rsqrt_fusion.1), kind=kOutput, calls=%fused_computation.92 | convolution fusion | flops 4304404480 | bytes 10498048 | tf_op jit(solution)/shard_map/dot_general | solution.py:98
  75.0 23.3 %fusion.107 = f32[8,128,8]{2,0,1:T(8,128)S(1)} fusion(f32[8,128,8]{2,0,1:T(8,128)S(1)} %copy.146), kind=kOutput, calls=%fused_computation.197 | output fusion | flops 1040384 | bytes 65536 | tf_op jit(solution)/shard_map/jit(cumsum)/reduce_window_sum | solution.py:117
  98.9 3.7 collective-permute-start
  102.6 3.8 convolution_convert_fusion.5
  107.3 2.1 collective-permute-start.1
  114.8 2.6 divide_multiply_fusion.1
  117.3 2.9 copy.144
  120.3 2.1 copy.201
  124.4 3.5 fusion.43
  129.5 19.8 %while.26 = (s32[]{:T(128)}, f32[8,64,128]{2,1,0:T(8,128)S(1)}, f32[8,8,64,128]{3,2,1,0:T(8,128)}, f32[8,8]{1,0:T(8,128)}, f32[8,8,64,128]{3,2,1,0:T(8,128)}, /*index=5*/s32[]{:T(128)}, s32[]{:T(128)}) while((s32[]{:T(128)}, f32[8,64,128]{2,1,0:T(8,128)S(1)}, f32[8,8,64,128]{3,2,1,0:T(8,128)}, f32[8,8]{1,0:T(8,128)}, ...), condition=%wide.region_3.4_spmd.clone, body=%wide.region_2.3_spmd.clone.sunk | while | flops 262147 | bytes 1311424 | solution.py:129
  153.1 7.8 %all-to-all-start = ((f32[32,1,8]{2,1,0:T(1,128)}), f32[32,1,8]{2,1,0:T(1,128)S(1)}, u32[]{:S(2)}, u32[]{:S(2)}) async-start(f32[32,1,8]{2,1,0:T(1,128)} %broadcast_in_dim.64), calls=%async_computation | async-start | bytes 32768 | tf_op jit(solution)/shard_map/all_to_all | solution.py:23
  164.7 2.4 reshape.291
  167.2 4.1 copy.159
  172.9 3.2 fusion.110
  176.1 9.7 %fusion.17 = f32[8,8,64,128]{3,2,1,0:T(8,128)} fusion(f32[8,128,8,64]{1,0,3,2:T(8,128)S(1)} %copy-done.18, f32[8,8,128]{2,1,0:T(8,128)S(1)} %copy.147, f32[8,128,128]{2,1,0:T(8,128)S(1)} %fusion.109, pred[128,128]{1,0:T(8,128)(4,1)S(1)} %iota_compare_fusion), kind=kOutput, calls=%fused_computation.30 | convolution fusion | flops 808452096 | bytes 4767744 | tf_op jit(solution)/shard_map/chqk,ckhp->cqhp/dot_general | solution.py:122
  185.7 11.7 %all-gather.10.cloned.1.call-done = bf16[256,64,128]{2,1,0:T(8,128)(2,1)} async-done(((bf16[8,64,128]{2,1,0:T(8,128)(2,1)}), bf16[256,64,128]{2,1,0:T(8,128)(2,1)}) %all-gather.10.cloned.1.call-update) | async-done | bytes 4194320 | tf_op jit(solution)/shard_map/all_gather | solution.py:82
  197.4 6.2 %fusion.10 = f32[8,1,64,128]{3,1,2,0:T(1,128)S(1)} fusion(f32[32,8,1,1]{0,2,3,1:T(1,128)S(1)} %copy.184, bf16[32,8,64,128]{3,2,1,0:T(8,128)(2,1)} %bitcast.226), kind=kOutput, calls=%fused_computation.23 | convolution fusion | flops 25165824 | bytes 4457472 | tf_op jit(solution)/shard_map/mh,mhpn->hpn/dot_general | solution.py:79
  203.7 5.1 fusion.42
  208.8 2.8 copy.192
  211.6 4.8 reshape.289
  216.7 1.9 copy.160
  218.6 8.5 %convolution_convert_fusion.1 = bf16[1024,2048]{1,0:T(8,128)(2,1)} fusion(bf16[2,512,2048]{2,1,0:T(8,128)(2,1)} %param.29, f32[1024,512]{1,0:T(8,128)} %copy.160, f32[1024,512]{1,0:T(8,128)} %reshape.289, f32[1024,512]{1,0:T(8,128)} %divide_multiply_fusion.1, f32[512]{0:T(512)S(1)} %bitcast.267, f32[512]{0:T(512)S(1)} %copy-done.39, ...), kind=kOutput, calls=%fused_computation.36 | convolution fusion | flops 2155347968 | bytes 13635584 | tf_op jit(solution)/shard_map/dot_general | solution.py:153
  227.8 4.4 sort.34
  232.2 4.5 gather_fusion
  238.1 3.6 all_to_all.38
  242.5 11.0 %all_to_all.39 = s32[16,2,1,32]{3,2,1,0:T(1,128)S(1)} all-to-all(s32[16,2,1,32]{3,2,1,0:T(1,128)S(1)} %copy.162), channel_id=1, replica_groups=mesh['seq_0'=4,'seq_1'=4,'seq_2'=2,'tp'=4] {'seq_0','seq_1'}, dimensions={0} | all-to-all | bytes 8192 | tf_op jit(solution)/shard_map/all_to_all | solution.py:46
  254.8 18.2 %reduce-scatter.3.cloned.1.call-done = bf16[1024,512]{1,0:T(8,128)(2,1)} async-done(((bf16[1024,2048]{1,0:T(8,128)(2,1)}), bf16[1024,512]{1,0:T(8,128)(2,1)}) %reduce-scatter.3.cloned.1.call-update) | async-done | bytes 1048592 | tf_op jit(solution)/shard_map/reduce_scatter | solution.py:161
  274.5 4.0 gather_fusion.1
  278.6 4.8 all_to_all.40
  284.5 6.7 %all-to-all-start.4 = ((bf16[16,2,1,32,512]{4,3,1,2,0:T(8,128)(2,1)}), bf16[16,2,1,32,512]{4,3,1,2,0:T(8,128)(2,1)S(1)}, u32[]{:S(2)}, u32[]{:S(2)}) async-start(bf16[16,2,1,32,512]{4,3,1,2,0:T(8,128)(2,1)} %copy.164), calls=%async_computation.5 | async-start | bytes 2097152 | tf_op jit(solution)/shard_map/all_to_all | solution.py:46
  291.2 4.4 sort.35
  295.6 11.9 %all-to-all-done.4 = bf16[16,2,1,32,512]{4,3,1,2,0:T(8,128)(2,1)S(1)} async-done(((bf16[16,2,1,32,512]{4,3,1,2,0:T(8,128)(2,1)}), bf16[16,2,1,32,512]{4,3,1,2,0:T(8,128)(2,1)S(1)}, u32[]{:S(2)}, u32[]{:S(2)}) %all-to-all-start.4) | async-done | bytes 1048608 | tf_op jit(solution)/shard_map/all_to_all | solution.py:46
  307.5 5.1 gather_fusion.2
  312.8 5.5 copy.202
  318.4 39.9 %all-gather.12.cloned.1.call-done = bf16[1024,2048]{1,0:T(8,128)(2,1)} async-done(((bf16[1024,512]{1,0:T(8,128)(2,1)}), bf16[1024,2048]{1,0:T(8,128)(2,1)}) %all-gather.12.cloned.1.call-update) | async-done | bytes 4194320 | tf_op jit(solution)/shard_map/all_gather | solution.py:157
  358.3 3.2 fusion.5
  363.7 3.7 collective-permute-start.3
  369.1 23.3 %fusion.108 = f32[8,128,8]{2,0,1:T(8,128)S(1)} fusion(f32[8,128,8]{2,0,1:T(8,128)S(1)} %copy.167), kind=kOutput, calls=%fused_computation.198 | output fusion | flops 1040384 | bytes 65536 | tf_op jit(solution)/shard_map/jit(cumsum)/reduce_window_sum | solution.py:117
  392.5 8.0 %convolution_convert_fusion.2 = bf16[1024,1024]{1,0:T(8,128)(2,1)S(1)} fusion(bf16[2048,1024]{1,0:T(8,128)(2,1)} %bitcast.230, bf16[1024,2048]{1,0:T(8,128)(2,1)} %all-gather.12.cloned.1.call-done, f32[2048]{0:T(1024)S(1)} %bitcast.254, f32[1024]{0:T(1024)S(1)} %add_rsqrt_fusion), kind=kOutput, calls=%fused_computation.91 | convolution fusion | flops 4304404480 | bytes 10498048 | tf_op jit(solution)/shard_map/dot_general | solution.py:98
  403.4 2.1 collective-permute-start.2
  409.2 2.6 divide_multiply_fusion
  411.7 2.9 copy.165
  414.7 2.1 copy.203
  416.7 1.7 broadcast_multiply_fusion
  418.7 3.5 fusion.36
  423.8 19.8 %while.27 = (s32[]{:T(128)}, f32[8,64,128]{2,1,0:T(8,128)S(1)}, f32[8,8,64,128]{3,2,1,0:T(8,128)}, f32[8,8]{1,0:T(8,128)}, f32[8,8,64,128]{3,2,1,0:T(8,128)}, /*index=5*/s32[]{:T(128)}, s32[]{:T(128)}) while((s32[]{:T(128)}, f32[8,64,128]{2,1,0:T(8,128)S(1)}, f32[8,8,64,128]{3,2,1,0:T(8,128)}, f32[8,8]{1,0:T(8,128)}, ...), condition=%wide.region_15.16_spmd.clone, body=%wide.region_14.15_spmd.clone.sunk | while | flops 262147 | bytes 1311424 | solution.py:129
  445.1 7.2 %all-to-all-start.5 = ((f32[32,1,8]{2,1,0:T(1,128)}), f32[32,1,8]{2,1,0:T(1,128)S(1)}, u32[]{:S(2)}, u32[]{:S(2)}) async-start(f32[32,1,8]{2,1,0:T(1,128)} %broadcast_in_dim.112), calls=%async_computation.6 | async-start | bytes 32768 | tf_op jit(solution)/shard_map/all_to_all | solution.py:23
  456.1 2.5 reshape.292
  458.6 4.3 copy.180
  464.5 3.2 fusion.112
  467.7 9.7 %fusion.12 = f32[8,8,64,128]{3,2,1,0:T(8,128)} fusion(f32[8,128,8,64]{1,0,3,2:T(8,128)S(1)} %copy-done.19, f32[8,8,128]{2,1,0:T(8,128)S(1)} %copy.168, f32[8,128,128]{2,1,0:T(8,128)S(1)} %fusion.111, pred[128,128]{1,0:T(8,128)(4,1)S(1)} %iota_compare_fusion), kind=kOutput, calls=%fused_computation.25 | convolution fusion | flops 808452096 | bytes 4767744 | tf_op jit(solution)/shard_map/chqk,ckhp->cqhp/dot_general | solution.py:122
  477.4 13.8 %all-gather.14.cloned.1.call-done = bf16[256,64,128]{2,1,0:T(8,128)(2,1)} async-done(((bf16[8,64,128]{2,1,0:T(8,128)(2,1)}), bf16[256,64,128]{2,1,0:T(8,128)(2,1)}) %all-gather.14.cloned.1.call-update) | async-done | bytes 4194320 | tf_op jit(solution)/shard_map/all_gather | solution.py:82
  491.1 6.0 %fusion.8 = f32[8,1,64,128]{3,1,2,0:T(1,128)S(1)} fusion(f32[32,8,1,1]{0,2,3,1:T(1,128)S(1)} %copy.189, bf16[32,8,64,128]{3,2,1,0:T(8,128)(2,1)} %bitcast.227), kind=kOutput, calls=%fused_computation.21 | convolution fusion | flops 25165824 | bytes 4457472 | tf_op jit(solution)/shard_map/mh,mhpn->hpn/dot_general | solution.py:79
  497.2 5.1 fusion.35
  502.3 2.7 copy.193
  505.0 4.8 reshape.290
  510.1 1.9 copy.181
  512.0 8.4 %convolution_convert_fusion = bf16[1024,2048]{1,0:T(8,128)(2,1)} fusion(bf16[2,512,2048]{2,1,0:T(8,128)(2,1)} %param.29, f32[1024,512]{1,0:T(8,128)} %copy.181, f32[1024,512]{1,0:T(8,128)} %reshape.290, f32[1024,512]{1,0:T(8,128)} %divide_multiply_fusion, f32[512]{0:T(512)S(1)} %bitcast.266, f32[512]{0:T(512)S(1)} %mul.565, bf16[1024,1024]{1,0:T(8,128)(2,1)} %copy-done.17), kind=kOutput, calls=%fused_computation.35 | convolution fusion | flops 2155347968 | bytes 13635584 | tf_op jit(solution)/shard_map/dot_general | solution.py:153
  520.5 45.8 %reduce-scatter.5.cloned.1.call-done = bf16[1024,512]{1,0:T(8,128)(2,1)} async-done(((bf16[1024,2048]{1,0:T(8,128)(2,1)}), bf16[1024,512]{1,0:T(8,128)(2,1)}) %reduce-scatter.5.cloned.1.call-update) | async-done | bytes 1048592 | tf_op jit(solution)/shard_map/reduce_scatter | solution.py:161
  566.3 2.5 add_convert_fusion
  (274 shorter events, 92.6 us)
Async XLA Ops:
  6.5 53.9 %all-gather.8.cloned.1.call-start = ((), (), s32[]{:S(2)}) async-start(), calls=%async_computation.8 | async-start | bytes 5242880 | tf_op jit(solution)/shard_map/all_gather | solution.py:157
  7.3 190.2 %all-gather.10.cloned.1.call-start = ((), (), s32[]{:S(2)}) async-start(), calls=%async_computation.11 | async-start | bytes 4325376 | tf_op jit(solution)/shard_map/all_gather | solution.py:82
  15.3 3.2 copy-start.45
  15.3 3.8 copy-start.46
  15.3 4.4 copy-start.28
  15.3 5.0 copy-start.24
  15.3 5.0 copy-start.25
  60.5 3.4 copy-start.14
  71.1 1.6 copy-start.16
  71.1 2.2 copy-start.50
  98.9 15.1 %collective-permute-start = (bf16[3,512]{1,0:T(4,128)(2,1)}, bf16[3,512]{1,0:T(4,128)(2,1)S(1)}, u32[]{:S(2)}, u32[]{:S(2)}) collective-permute-start(bf16[3,512]{1,0:T(4,128)(2,1)} %slice.314), channel_id=1, source_target_pairs={{0,4},{4,8},{8,12},{12,16},{16,20},{20,24},{24,28},{28,32},{32,36}... | collective-permute-start | bytes 9224 | tf_op jit(solution)/shard_map/ppermute | solution.py:33
  106.4 0.8 copy-start.23
  106.4 5.4 copy-start.34
  106.4 5.4 copy-start.35
  107.3 3.4 collective-permute-start.1
  113.0 1.4 copy-start.12
  122.3 2.0 copy-start.1
  122.3 2.0 copy-start.7
  129.5 20.5 %copy-start.47 = (f32[2,8]{1,0:T(2,128)S(1)}, f32[2,8]{1,0:T(2,128)}, u32[]{:S(2)}) copy-start(f32[2,8]{1,0:T(2,128)} %param.27) | copy-start | bytes 196
  129.5 22.3 %copy-start.37 = (f32[2,512]{1,0:T(2,128)S(1)}, f32[2,512]{1,0:T(2,128)}, u32[]{:S(2)}) copy-start(f32[2,512]{1,0:T(2,128)} %param.28) | copy-start | bytes 12292
  150.5 2.6 copy-start.41
  153.1 18.2 %all-to-all-start = ((f32[32,1,8]{2,1,0:T(1,128)}), f32[32,1,8]{2,1,0:T(1,128)S(1)}, u32[]{:S(2)}, u32[]{:S(2)}) async-start(f32[32,1,8]{2,1,0:T(1,128)} %broadcast_in_dim.64), calls=%async_computation | async-start | bytes 32768 | tf_op jit(solution)/shard_map/all_to_all | solution.py:23
  160.9 112.1 %reduce-scatter.3.cloned.1.call-start = ((), (), s32[]{:S(2)}) async-start(), calls=%async_computation.9 | async-start | bytes 5242880 | tf_op jit(solution)/shard_map/reduce_scatter | solution.py:161
  167.2 4.2 copy-start.26
  167.2 4.5 copy-start.8
  167.2 5.7 copy-start.5
  172.9 3.2 copy-start.18
  197.4 6.3 %copy-start.2 = (f32[64,8,8,128]{3,2,1,0:T(8,128)S(1)}, f32[64,8,8,128]{3,2,1,0:T(8,128)}, u32[]{:S(2)}) copy-start(f32[64,8,8,128]{3,2,1,0:T(8,128)} %copy-done.1) | copy-start | bytes 6291460
  197.4 6.3 %copy-start.21 = (f32[8,128,8,64]{1,3,2,0:T(8,128)S(1)}, f32[8,128,8,64]{1,3,2,0:T(8,128)}, u32[]{:S(2)}) copy-start(f32[8,128,8,64]{1,3,2,0:T(8,128)} %copy.159) | copy-start | bytes 6291460
  197.4 6.3 %copy-start.42 = (f32[8]{0:T(128)S(1)}, f32[8]{0:T(128)}, u32[]{:S(2)}) copy-start(f32[8]{0:T(128)} %copy-done.41) | copy-start | bytes 100
  216.7 1.9 copy-start.39
  216.7 1.9 copy-start.44
  232.2 40.8 %copy-start.11 = (bf16[1024,512]{1,0:T(8,128)(2,1)S(1)}, bf16[1024,512]{1,0:T(8,128)(2,1)}, u32[]{:S(2)}) copy-start(bf16[1024,512]{1,0:T(8,128)(2,1)} %param.17) | copy-start | bytes 3145732
  284.5 23.0 %all-to-all-start.4 = ((bf16[16,2,1,32,512]{4,3,1,2,0:T(8,128)(2,1)}), bf16[16,2,1,32,512]{4,3,1,2,0:T(8,128)(2,1)S(1)}, u32[]{:S(2)}, u32[]{:S(2)}) async-start(bf16[16,2,1,32,512]{4,3,1,2,0:T(8,128)(2,1)} %copy.164), calls=%async_computation.5 | async-start | bytes 2097152 | tf_op jit(solution)/shard_map/all_to_all | solution.py:46
  291.2 67.1 %all-gather.12.cloned.1.call-start = ((), (), s32[]{:S(2)}) async-start(), calls=%async_computation.12 | async-start | bytes 5242880 | tf_op jit(solution)/shard_map/all_gather | solution.py:157
  312.6 178.5 %all-gather.14.cloned.1.call-start = ((), (), s32[]{:S(2)}) async-start(), calls=%async_computation.13 | async-start | bytes 4325376 | tf_op jit(solution)/shard_map/all_gather | solution.py:82
  312.8 48.7 %copy-start.49 = (bf16[2,2048,256]{2,1,0:T(8,128)(2,1)S(1)}, bf16[2,2048,256]{2,1,0:T(8,128)(2,1)}, u32[]{:S(2)}) copy-start(bf16[2,2048,256]{2,1,0:T(8,128)(2,1)} %param.21) | copy-start | bytes 6291460
  318.4 43.2 %copy-start.29 = (f32[1,2048]{1,0:T(1,128)S(1)}, f32[1,2048]{1,0:T(1,128)}, u32[]{:S(2)}) copy-start(f32[1,2048]{1,0:T(1,128)} %get-tuple-element.155) | copy-start | bytes 24580
  358.3 3.4 copy-start.15
  361.8 5.7 copy-start.48
  361.8 5.7 copy-start.51
  363.1 5.7 copy-start.22
  363.7 41.9 %collective-permute-start.3 = (bf16[3,256]{1,0:T(4,128)(2,1)}, bf16[3,256]{1,0:T(4,128)(2,1)}, u32[]{:S(2)}, u32[]{:S(2)}) collective-permute-start(bf16[3,256]{1,0:T(4,128)(2,1)} %slice.336), channel_id=1, source_target_pairs={{0,4},{4,8},{8,12},{12,16},{16,20},{20,24},{24,28},{28,32},{32,36}... | collective-permute-start | bytes 4616 | tf_op jit(solution)/shard_map/ppermute | solution.py:33
  367.4 1.3 copy-start.38
  400.5 2.1 copy-start.17
  402.0 4.7 copy-start.30
  402.0 4.8 copy-start.31
  402.0 4.8 copy-start.32
  402.0 4.8 copy-start.33
  403.4 4.9 collective-permute-start.2
  407.4 1.4 copy-start.13
  416.7 2.0 copy-start.3
  416.7 2.0 copy-start.9
  423.8 20.5 %copy-start.40 = (f32[8]{0:T(128)S(1)}, f32[8]{0:T(128)}, u32[]{:S(2)}) copy-start(f32[8]{0:T(128)} %get-tuple-element.169) | copy-start | bytes 100
  445.1 17.9 %all-to-all-start.5 = ((f32[32,1,8]{2,1,0:T(1,128)}), f32[32,1,8]{2,1,0:T(1,128)S(1)}, u32[]{:S(2)}, u32[]{:S(2)}) async-start(f32[32,1,8]{2,1,0:T(1,128)} %broadcast_in_dim.112), calls=%async_computation.6 | async-start | bytes 32768 | tf_op jit(solution)/shard_map/all_to_all | solution.py:23
  452.3 114.0 %reduce-scatter.5.cloned.1.call-start = ((), (), s32[]{:S(2)}) async-start(), calls=%async_computation.10 | async-start | bytes 5242880 | tf_op jit(solution)/shard_map/reduce_scatter | solution.py:161
  458.6 4.4 copy-start.27
  458.6 4.7 copy-start.10
  458.6 5.9 %copy-start.6 = (f32[8,8,64,128]{3,2,1,0:T(8,128)S(1)}, f32[8,8,64,128]{3,2,1,0:T(8,128)}, u32[]{:S(2)}) copy-start(f32[8,8,64,128]{3,2,1,0:T(8,128)} %get-tuple-element.67) | copy-start | bytes 6291460
  464.5 3.2 copy-start.19
  491.1 6.0 %copy-start.4 = (f32[64,8,8,128]{3,2,1,0:T(8,128)S(1)}, f32[64,8,8,128]{3,2,1,0:T(8,128)}, u32[]{:S(2)}) copy-start(f32[64,8,8,128]{3,2,1,0:T(8,128)} %copy-done.3) | copy-start | bytes 6291460
  491.1 6.0 %copy-start.20 = (f32[8,128,8,64]{1,3,2,0:T(8,128)S(1)}, f32[8,128,8,64]{1,3,2,0:T(8,128)}, u32[]{:S(2)}) copy-start(f32[8,128,8,64]{1,3,2,0:T(8,128)} %copy.180) | copy-start | bytes 6291460
  510.1 1.9 copy-start.43
  520.5 45.9 %copy-start = (bf16[1024,512]{1,0:T(8,128)(2,1)S(1)}, bf16[1024,512]{1,0:T(8,128)(2,1)}, u32[]{:S(2)}) copy-start(bf16[1024,512]{1,0:T(8,128)(2,1)} %gather_fusion.2) | copy-start | bytes 3145732
  (1 other events, 0.7 us)
Sparse Core Ops, SparseCore 0:
  9.0 51.3 all-gather.7
  150.1 47.2 all-gather.9
  227.2 45.7 reduce-scatter.2
  312.7 45.5 all-gather.11
  444.4 46.7 all-gather.13
  520.6 45.6 reduce-scatter.4
where the time goes:
time: 584 us; the launch traced here: 576 us
  waiting for transfers between devices  183 us (31%)
  other arithmetic  118 us (20%)
  local copies, waits for them, and re-layouts  110 us (19%)
  matrix products  97.5 us (17%)
  starting transfers between devices  33.7 us (6%)
  blocking collectives  19.4 us (3%)
  between operations  14.5 us (2%)
    all_gather x2, waiting for transfers between devices, spread_features(): return lax.all_gather(piece, 'tp', axis=1, tiled=True)  79.5 us
    reduce_scatter x2, waiting for transfers between devices, collect_heads(): lax.psum_scatter(partial_sum.astype(jnp.bfloat16), 'tp', scatter_dimensio...  64.1 us
    another operation x2, other arithmetic, mixer(): cumul = jnp.cumsum(log_blocks, axis=1)  46.6 us
    all_gather x2, waiting for transfers between devices, incoming_state(): lax.all_gather(local_end[None].astype(jnp.bfloat16), SEQ, axis=0, tiled=T...  25.5 us
    all_to_all x3, blocking collectives, moved_by_axis(): lax.all_to_all(blocks, axes[k], split_axis=k, concat_axis=k, tiled=True)  19.4 us
    dot_general x2, matrix products, mixer(): jnp.einsum('chqk,ckhp->cqhp', intersection[:, None] * jnp.exp(spread), fe...  19.3 us
    dot_general x2, matrix products, mixer(): jnp.dot(mixed_heads, w_out[which], preferred_element_type=jnp.float32)  17 us
    unnamed x111, local copies, waits for them, and re-layouts  16.7 us
  transfers between devices with their start and end apart: 13, of which 8 were waited for; matrix products, arithmetic and copies ran while one was open for 24% of the time, Pallas kernels for 0%

commit v1 on v0

--- a/solution.py
+++ b/solution.py
@@ -79,9 +79,12 @@
     return jnp.zeros(local_end.shape, jnp.float32) + jnp.einsum(
         "mh,mhpn->hpn",
         factors,
-        lax.all_gather(local_end[None].astype(jnp.bfloat16), SEQ, axis=0, tiled=True).astype(
-            jnp.float32
-        ),
+        jnp.concatenate(
+            lax.all_to_all(
+                jnp.stack([local_end[None].astype(jnp.bfloat16)] * lax.axis_size(SEQ)), SEQ, 0, 0
+            ),
+            axis=0,
+        ).astype(jnp.float32),
         precision=highest,
     )
 

time: 584 us -> 623 us (1.067)
  waiting for transfers between devices: 183 us -> 201 us
  starting transfers between devices: 33.7 us -> 48.2 us
    all_to_all x0 -> x2, waiting for transfers between devices: none -> 46.9 us  [incoming_state(): lax.all_to_all(jnp.stack([local_end[None].astype(jnp.bfloat16)] * lax.axi...]
    all_gather x2 -> x0, waiting for transfers between devices: 25.5 us -> none  [incoming_state(): lax.all_gather(local_end[None].astype(jnp.bfloat16), SEQ, axis=0, tiled=T...]
    all_to_all x0 -> x2, starting transfers between devices: none -> 15.1 us  [incoming_state(): lax.all_to_all(jnp.stack([local_end[None].astype(jnp.bfloat16)] * lax.axi...]
    another operation x2 -> x4, local copies, waits for them, and re-layouts: 3.21 us -> 9.44 us  [the longest x2 6.16 us: incoming_state(): jnp.stack([local_end[None].astype(jnp.bfloat16)] * lax.axis_size(SEQ))]
    unnamed x111 -> x127, local copies, waits for them, and re-layouts: 16.7 us -> 17.4 us
  transfers between devices with their start and end apart: 13 -> 13, of which waited for: 8 -> 7; matrix products, arithmetic and copies ran while one was open for 24% -> 27% of each run, Pallas kernels for 0% -> 0%
where the time goes in v1:
time: 623 us; the launch traced here: 614 us
  waiting for transfers between devices  201 us (32%)
  other arithmetic  118 us (19%)
  local copies, waits for them, and re-layouts  112 us (18%)
  matrix products  98.9 us (16%)
  starting transfers between devices  48.2 us (8%)
  blocking collectives  20.7 us (3%)
  between operations  14.3 us (2%)
    all_gather x2, waiting for transfers between devices, spread_features(): return lax.all_gather(piece, 'tp', axis=1, tiled=True)  79.3 us
    reduce_scatter x2, waiting for transfers between devices, collect_heads(): lax.psum_scatter(partial_sum.astype(jnp.bfloat16), 'tp', scatter_dimensio...  62.5 us
    all_to_all x2, waiting for transfers between devices, incoming_state(): lax.all_to_all(jnp.stack([local_end[None].astype(jnp.bfloat16)] * lax.axi...  46.9 us
    another operation x2, other arithmetic, mixer(): cumul = jnp.cumsum(log_blocks, axis=1)  46.6 us
    all_to_all x3, blocking collectives, moved_by_axis(): lax.all_to_all(blocks, axes[k], split_axis=k, concat_axis=k, tiled=True)  20.7 us
    dot_general x2, matrix products, mixer(): jnp.einsum('chqk,ckhp->cqhp', intersection[:, None] * jnp.exp(spread), fe...  19.3 us
    unnamed x127, local copies, waits for them, and re-layouts  17.4 us
    dot_general x2, matrix products, mixer(): jnp.dot(mixed_heads, w_out[which], preferred_element_type=jnp.float32)  17 us
  transfers between devices with their start and end apart: 13, of which 7 were waited for; matrix products, arithmetic and copies ran while one was open for 27% of the time, Pallas kernels for 0%

profile of v1, /device:TPU:1, one launch (start us, length us, event | category | flops | bytes accessed | tf_op | source)
XLA Modules:
  0.0 614.0 jit_solution(7257256603297625840)
XLA Ops:
  7.3 8.0 %fusion.98 = (bf16[1,2048,2,512]{3,2,1,0:T(2,128)(2,1)}, bf16[1,2048,2,512]{3,2,1,0:T(2,128)(2,1)S(1)}) fusion(bf16[2,2048,2,512]{3,2,1,0:T(2,128)(2,1)} %param.20), kind=kLoop, calls=%fused_computation.187 | loop fusion | bytes 16777216 | tf_op jit(solution)/shard_map/slice | solution.py:102
  15.3 3.2 copy.200
  21.5 39.0 %all-gather.4.cloned.1.call-done = bf16[1024,2048]{1,0:T(8,128)(2,1)} async-done(((bf16[1024,512]{1,0:T(8,128)(2,1)}), bf16[1024,2048]{1,0:T(8,128)(2,1)}) %all-gather.4.cloned.1.call-update) | async-done | bytes 4194320 | tf_op jit(solution)/shard_map/all_gather | solution.py:160
  60.5 3.2 fusion.2
  63.9 7.2 %convolution_convert_fusion.3 = bf16[1024,1024]{1,0:T(8,128)(2,1)S(1)} fusion(bf16[2048,1024]{1,0:T(8,128)(2,1)} %bitcast.227, bf16[1024,2048]{1,0:T(8,128)(2,1)S(1)} %copy-done.14, f32[2048]{0:T(1024)S(1)} %bitcast.253, f32[1024]{0:T(1024)S(1)} %add_rsqrt_fusion.1), kind=kOutput, calls=%fused_computation.92 | convolution fusion | flops 4304404480 | bytes 10498048 | tf_op jit(solution)/shard_map/dot_general | solution.py:101
  75.1 23.3 %fusion.107 = f32[8,128,8]{2,0,1:T(8,128)S(1)} fusion(f32[8,128,8]{2,0,1:T(8,128)S(1)} %copy.146), kind=kOutput, calls=%fused_computation.197 | output fusion | flops 1040384 | bytes 65536 | tf_op jit(solution)/shard_map/jit(cumsum)/reduce_window_sum | solution.py:120
  99.0 3.7 collective-permute-start
  102.8 3.5 convolution_convert_fusion.5
  111.1 7.5 %all-to-all-start = ((f32[32,1,8]{2,1,0:T(1,128)}), f32[32,1,8]{2,1,0:T(1,128)S(1)}, u32[]{:S(2)}, u32[]{:S(2)}) async-start(f32[32,1,8]{2,1,0:T(1,128)} %broadcast_in_dim.64), calls=%async_computation | async-start | bytes 32768 | tf_op jit(solution)/shard_map/all_to_all | solution.py:23
  122.8 2.6 divide_multiply_fusion.1
  125.4 2.9 copy.144
  128.3 2.1 copy.201
  132.5 3.5 fusion.43
  137.6 19.8 %while.26 = (s32[]{:T(128)}, f32[8,64,128]{2,1,0:T(8,128)S(1)}, f32[8,8,64,128]{3,2,1,0:T(8,128)}, f32[8,8]{1,0:T(8,128)}, f32[8,8,64,128]{3,2,1,0:T(8,128)}, /*index=5*/s32[]{:T(128)}, s32[]{:T(128)}) while((s32[]{:T(128)}, f32[8,64,128]{2,1,0:T(8,128)S(1)}, f32[8,8,64,128]{3,2,1,0:T(8,128)}, f32[8,8]{1,0:T(8,128)}, ...), condition=%wide.region_3.4_spmd.clone, body=%wide.region_2.3_spmd.clone.sunk | while | flops 262147 | bytes 1311424 | solution.py:132
  157.5 3.1 stack.4
  160.6 7.6 %all-to-all-start.1 = ((bf16[32,1,8,64,128]{4,3,2,1,0:T(8,128)(2,1)}), bf16[32,1,8,64,128]{4,3,2,1,0:T(8,128)(2,1)}, u32[]{:S(2)}, u32[]{:S(2)}) async-start(bf16[32,1,8,64,128]{4,3,2,1,0:T(8,128)(2,1)} %stack.4), calls=%async_computation.1 | async-start | bytes 8388608 | tf_op jit(solution)/shard_map/all_to_all | solution.py:83
  174.5 2.4 reshape.303
  176.9 4.1 copy.159
  183.2 3.1 fusion.110
  186.4 9.6 %fusion.17 = f32[8,8,64,128]{3,2,1,0:T(8,128)} fusion(f32[8,128,8,64]{1,0,3,2:T(8,128)S(1)} %copy-done.18, f32[8,8,128]{2,1,0:T(8,128)S(1)} %copy.147, f32[8,128,128]{2,1,0:T(8,128)S(1)} %fusion.109, pred[128,128]{1,0:T(8,128)(4,1)S(1)} %copy-done.28), kind=kOutput, calls=%fused_computation.30 | convolution fusion | flops 808452096 | bytes 4767744 | tf_op jit(solution)/shard_map/chqk,ckhp->cqhp/dot_general | solution.py:125
  196.0 22.4 %all-to-all-done.1 = bf16[32,1,8,64,128]{4,3,2,1,0:T(8,128)(2,1)} async-done(((bf16[32,1,8,64,128]{4,3,2,1,0:T(8,128)(2,1)}), bf16[32,1,8,64,128]{4,3,2,1,0:T(8,128)(2,1)}, u32[]{:S(2)}, u32[]{:S(2)}) %all-to-all-start.1) | async-done | bytes 4194336 | tf_op jit(solution)/shard_map/all_to_all | solution.py:83
  218.4 6.2 %fusion.10 = f32[8,1,64,128]{3,1,2,0:T(1,128)S(1)} fusion(f32[32,8,1,1]{0,2,3,1:T(1,128)S(1)} %copy.184, bf16[32,8,64,128]{3,2,1,0:T(8,128)(2,1)} %bitcast.29), kind=kOutput, calls=%fused_computation.23 | convolution fusion | flops 25165824 | bytes 4457472 | tf_op jit(solution)/shard_map/mh,mhpn->hpn/dot_general | solution.py:79
  224.7 5.1 fusion.42
  229.8 2.8 copy.192
  232.6 4.8 reshape.301
  239.6 8.5 %convolution_convert_fusion.1 = bf16[1024,2048]{1,0:T(8,128)(2,1)} fusion(bf16[2,512,2048]{2,1,0:T(8,128)(2,1)} %param.29, f32[1024,512]{1,0:T(8,128)} %copy.160, f32[1024,512]{1,0:T(8,128)} %reshape.301, f32[1024,512]{1,0:T(8,128)} %divide_multiply_fusion.1, f32[512]{0:T(512)S(1)} %bitcast.265, f32[512]{0:T(512)S(1)} %copy-done.45, ...), kind=kOutput, calls=%fused_computation.36 | convolution fusion | flops 2155347968 | bytes 13635584 | tf_op jit(solution)/shard_map/dot_general | solution.py:156
  248.8 4.4 sort.34
  253.1 4.5 gather_fusion
  259.1 6.9 %all_to_all.48 = s32[2,1,512]{2,1,0:T(1,128)S(1)} all-to-all(s32[2,1,512]{2,1,0:T(1,128)S(1)} %reshape.314), channel_id=1, replica_groups=mesh['seq_0'=4,'seq_1'=4,'seq_2'=2,'tp'=4] {'seq_2'}, dimensions={0} | all-to-all | bytes 8192 | tf_op jit(solution)/shard_map/all_to_all | solution.py:46
  266.7 9.0 %all_to_all.49 = s32[16,2,1,32]{3,2,1,0:T(1,128)S(1)} all-to-all(s32[16,2,1,32]{3,2,1,0:T(1,128)S(1)} %copy.162), channel_id=1, replica_groups=mesh['seq_0'=4,'seq_1'=4,'seq_2'=2,'tp'=4] {'seq_0','seq_1'}, dimensions={0} | all-to-all | bytes 8192 | tf_op jit(solution)/shard_map/all_to_all | solution.py:46
  277.1 16.8 %reduce-scatter.3.cloned.1.call-done = bf16[1024,512]{1,0:T(8,128)(2,1)} async-done(((bf16[1024,2048]{1,0:T(8,128)(2,1)}), bf16[1024,512]{1,0:T(8,128)(2,1)}) %reduce-scatter.3.cloned.1.call-update) | async-done | bytes 1048592 | tf_op jit(solution)/shard_map/reduce_scatter | solution.py:164
  295.4 4.0 gather_fusion.1
  299.5 4.8 all_to_all.50
  305.4 6.7 %all-to-all-start.5 = ((bf16[16,2,1,32,512]{4,3,1,2,0:T(8,128)(2,1)}), bf16[16,2,1,32,512]{4,3,1,2,0:T(8,128)(2,1)S(1)}, u32[]{:S(2)}, u32[]{:S(2)}) async-start(bf16[16,2,1,32,512]{4,3,1,2,0:T(8,128)(2,1)} %copy.164), calls=%async_computation.6 | async-start | bytes 2097152 | tf_op jit(solution)/shard_map/all_to_all | solution.py:46
  312.1 4.4 sort.35
  316.5 11.9 %all-to-all-done.5 = bf16[16,2,1,32,512]{4,3,1,2,0:T(8,128)(2,1)S(1)} async-done(((bf16[16,2,1,32,512]{4,3,1,2,0:T(8,128)(2,1)}), bf16[16,2,1,32,512]{4,3,1,2,0:T(8,128)(2,1)S(1)}, u32[]{:S(2)}, u32[]{:S(2)}) %all-to-all-start.5) | async-done | bytes 1048608 | tf_op jit(solution)/shard_map/all_to_all | solution.py:46
  328.4 5.2 gather_fusion.2
  333.7 5.4 copy.202
  339.0 40.3 %all-gather.6.cloned.1.call-done = bf16[1024,2048]{1,0:T(8,128)(2,1)} async-done(((bf16[1024,512]{1,0:T(8,128)(2,1)}), bf16[1024,2048]{1,0:T(8,128)(2,1)}) %all-gather.6.cloned.1.call-update) | async-done | bytes 4194320 | tf_op jit(solution)/shard_map/all_gather | solution.py:160
  379.4 3.2 fusion.5
  382.8 7.2 %convolution_convert_fusion.2 = bf16[1024,1024]{1,0:T(8,128)(2,1)S(1)} fusion(bf16[2048,1024]{1,0:T(8,128)(2,1)} %bitcast.228, bf16[1024,2048]{1,0:T(8,128)(2,1)S(1)} %copy-done.15, f32[2048]{0:T(1024)S(1)} %bitcast.250, f32[1024]{0:T(1024)S(1)} %add_rsqrt_fusion), kind=kOutput, calls=%fused_computation.91 | convolution fusion | flops 4304404480 | bytes 10498048 | tf_op jit(solution)/shard_map/dot_general | solution.py:101
  393.4 23.3 %fusion.108 = f32[8,128,8]{2,0,1:T(8,128)S(1)} fusion(f32[8,128,8]{2,0,1:T(8,128)S(1)} %copy.167), kind=kOutput, calls=%fused_computation.198 | output fusion | flops 1040384 | bytes 65536 | tf_op jit(solution)/shard_map/jit(cumsum)/reduce_window_sum | solution.py:120
  416.7 3.8 convolution_convert_fusion.4
  421.3 3.7 collective-permute-start.3
  428.5 7.6 %all-to-all-start.6 = ((f32[32,1,8]{2,1,0:T(1,128)}), f32[32,1,8]{2,1,0:T(1,128)S(1)}, u32[]{:S(2)}, u32[]{:S(2)}) async-start(f32[32,1,8]{2,1,0:T(1,128)} %broadcast_in_dim.112), calls=%async_computation.7 | async-start | bytes 32768 | tf_op jit(solution)/shard_map/all_to_all | solution.py:23
  439.7 2.5 divide_multiply_fusion
  442.2 2.9 copy.165
  445.1 2.1 copy.203
  449.2 3.5 fusion.36
  454.4 14.4 %while.27 = (s32[]{:T(128)}, f32[8,64,128]{2,1,0:T(8,128)S(1)}, f32[8,8,64,128]{3,2,1,0:T(8,128)}, f32[8,8]{1,0:T(8,128)S(1)}, f32[8,8,64,128]{3,2,1,0:T(8,128)}, /*index=5*/s32[]{:T(128)}, s32[]{:T(128)}) while((s32[]{:T(128)}, f32[8,64,128]{2,1,0:T(8,128)S(1)}, f32[8,8,64,128]{3,2,1,0:T(8,128)}, f32[8,8]{1,0:T(8,128)S(1)}, ...), condition=%wide.region_15.16_spmd.clone, body=%wide.region_14.15_spmd.clone.sunk | while | flops 262147 | bytes 1311424 | solution.py:132
  468.8 3.1 stack.5
  471.9 7.6 %all-to-all-start.7 = ((bf16[32,1,8,64,128]{4,3,2,1,0:T(8,128)(2,1)}), bf16[32,1,8,64,128]{4,3,2,1,0:T(8,128)(2,1)}, u32[]{:S(2)}, u32[]{:S(2)}) async-start(bf16[32,1,8,64,128]{4,3,2,1,0:T(8,128)(2,1)} %stack.5), calls=%async_computation.8 | async-start | bytes 8388608 | tf_op jit(solution)/shard_map/all_to_all | solution.py:83
  484.1 2.4 reshape.304
  486.5 4.3 copy.180
  492.4 3.2 fusion.112
  495.6 9.7 %fusion.12 = f32[8,8,64,128]{3,2,1,0:T(8,128)} fusion(f32[8,128,8,64]{1,0,3,2:T(8,128)S(1)} %copy-done.19, f32[8,8,128]{2,1,0:T(8,128)S(1)} %copy.168, f32[8,128,128]{2,1,0:T(8,128)S(1)} %fusion.111, pred[128,128]{1,0:T(8,128)(4,1)S(1)} %copy-done.29), kind=kOutput, calls=%fused_computation.25 | convolution fusion | flops 808452096 | bytes 4767744 | tf_op jit(solution)/shard_map/chqk,ckhp->cqhp/dot_general | solution.py:125
  505.3 24.5 %all-to-all-done.7 = bf16[32,1,8,64,128]{4,3,2,1,0:T(8,128)(2,1)} async-done(((bf16[32,1,8,64,128]{4,3,2,1,0:T(8,128)(2,1)}), bf16[32,1,8,64,128]{4,3,2,1,0:T(8,128)(2,1)}, u32[]{:S(2)}, u32[]{:S(2)}) %all-to-all-start.7) | async-done | bytes 4194336 | tf_op jit(solution)/shard_map/all_to_all | solution.py:83
  529.7 6.0 fusion.8
  535.8 5.1 fusion.35
  540.9 2.7 copy.193
  543.7 4.8 reshape.302
  550.7 8.5 %convolution_convert_fusion = bf16[1024,2048]{1,0:T(8,128)(2,1)} fusion(bf16[2,512,2048]{2,1,0:T(8,128)(2,1)} %param.29, f32[1024,512]{1,0:T(8,128)} %copy.181, f32[1024,512]{1,0:T(8,128)} %reshape.302, f32[1024,512]{1,0:T(8,128)} %divide_multiply_fusion, f32[512]{0:T(512)S(1)} %bitcast.264, f32[512]{0:T(512)S(1)} %copy-done.46, ...), kind=kOutput, calls=%fused_computation.35 | convolution fusion | flops 2155347968 | bytes 13635584 | tf_op jit(solution)/shard_map/dot_general | solution.py:156
  559.1 45.7 %reduce-scatter.5.cloned.1.call-done = bf16[1024,512]{1,0:T(8,128)(2,1)} async-done(((bf16[1024,2048]{1,0:T(8,128)(2,1)}), bf16[1024,512]{1,0:T(8,128)(2,1)}) %reduce-scatter.5.cloned.1.call-update) | async-done | bytes 1048592 | tf_op jit(solution)/shard_map/reduce_scatter | solution.py:164
  604.8 2.5 add_convert_fusion
  (290 shorter events, 95.8 us)
Async XLA Ops:
  6.5 53.9 %all-gather.4.cloned.1.call-start = ((), (), s32[]{:S(2)}) async-start(), calls=%async_computation.10 | async-start | bytes 5242880 | tf_op jit(solution)/shard_map/all_gather | solution.py:160
  15.2 3.2 copy-start.53
  15.2 3.8 copy-start.54
  15.2 4.4 copy-start.36
  15.2 5.0 copy-start.26
  15.3 5.6 copy-start.27
  60.5 3.4 copy-start.14
  71.1 1.7 copy-start.16
  71.1 2.3 copy-start.58
  75.1 27.7 %copy-start.57 = (bf16[2,2048,256]{2,1,0:T(8,128)(2,1)S(1)}, bf16[2,2048,256]{2,1,0:T(8,128)(2,1)}, u32[]{:S(2)}) copy-start(bf16[2,2048,256]{2,1,0:T(8,128)(2,1)} %param.21) | copy-start | bytes 6291460
  99.0 23.0 %collective-permute-start = (bf16[3,512]{1,0:T(4,128)(2,1)}, bf16[3,512]{1,0:T(4,128)(2,1)S(1)}, u32[]{:S(2)}, u32[]{:S(2)}) collective-permute-start(bf16[3,512]{1,0:T(4,128)(2,1)} %slice.314), channel_id=1, source_target_pairs={{0,4},{4,8},{8,12},{12,16},{16,20},{20,24},{24,28},{28,32},{32,36}... | collective-permute-start | bytes 9224 | tf_op jit(solution)/shard_map/ppermute | solution.py:33
  107.7 10.9 %collective-permute-start.1 = (bf16[3,256]{1,0:T(4,128)(2,1)}, bf16[3,256]{1,0:T(4,128)(2,1)}, u32[]{:S(2)}, u32[]{:S(2)}) collective-permute-start(bf16[3,256]{1,0:T(4,128)(2,1)} %slice.320), channel_id=1, source_target_pairs={{0,4},{4,8},{8,12},{12,16},{16,20},{20,24},{24,28},{28,32},{32,36}... | collective-permute-start | bytes 4616 | tf_op jit(solution)/shard_map/ppermute | solution.py:33
  111.1 46.4 %all-to-all-start = ((f32[32,1,8]{2,1,0:T(1,128)}), f32[32,1,8]{2,1,0:T(1,128)S(1)}, u32[]{:S(2)}, u32[]{:S(2)}) async-start(f32[32,1,8]{2,1,0:T(1,128)} %broadcast_in_dim.64), calls=%async_computation | async-start | bytes 32768 | tf_op jit(solution)/shard_map/all_to_all | solution.py:23
  121.1 1.4 copy-start.13
  130.4 2.1 copy-start.1
  130.4 2.1 copy-start.7
  160.5 7.6 %copy-start.55 = (f32[2,8]{1,0:T(2,128)S(1)}, f32[2,8]{1,0:T(2,128)}, u32[]{:S(2)}) copy-start(f32[2,8]{1,0:T(2,128)} %param.27) | copy-start | bytes 196
  160.6 9.6 %copy-start.43 = (f32[2,512]{1,0:T(2,128)S(1)}, f32[2,512]{1,0:T(2,128)}, u32[]{:S(2)}) copy-start(f32[2,512]{1,0:T(2,128)} %param.28) | copy-start | bytes 12292
  160.6 10.4 %copy-start.24 = (f32[8,8]{1,0:T(8,128)S(1)}, f32[8,8]{1,0:T(8,128)}, u32[]{:S(2)}) copy-start(f32[8,8]{1,0:T(8,128)} %get-tuple-element.145) | copy-start | bytes 772
  160.6 57.8 %all-to-all-start.1 = ((bf16[32,1,8,64,128]{4,3,2,1,0:T(8,128)(2,1)}), bf16[32,1,8,64,128]{4,3,2,1,0:T(8,128)(2,1)}, u32[]{:S(2)}, u32[]{:S(2)}) async-start(bf16[32,1,8,64,128]{4,3,2,1,0:T(8,128)(2,1)} %stack.4), calls=%async_computation.1 | async-start | bytes 8388608 | tf_op jit(solution)/shard_map/all_to_all | solution.py:83
  168.1 125.8 %reduce-scatter.3.cloned.1.call-start = ((), (), s32[]{:S(2)}) async-start(), calls=%async_computation.11 | async-start | bytes 5242880 | tf_op jit(solution)/shard_map/reduce_scatter | solution.py:164
  168.8 8.1 %copy-start.49 = (f32[8]{0:T(128)}, f32[8]{0:T(128)S(1)}, u32[]{:S(2)}) copy-start(f32[8]{0:T(128)S(1)} %get-tuple-element.170) | copy-start | bytes 100
  169.5 11.6 %copy-start.34 = (pred[32]{0:T(512)(128)(4,1)}, pred[32]{0:T(512)(128)(4,1)S(1)}, u32[]{:S(2)}) copy-start(pred[32]{0:T(512)(128)(4,1)S(1)} %iota_compare_fusion.1) | copy-start | bytes 100
  176.9 5.1 copy-start.8
  176.9 6.3 %copy-start.5 = (f32[8,8,64,128]{3,2,1,0:T(8,128)S(1)}, f32[8,8,64,128]{3,2,1,0:T(8,128)}, u32[]{:S(2)}) copy-start(f32[8,8,64,128]{3,2,1,0:T(8,128)} %get-tuple-element.63) | copy-start | bytes 6291460
  183.2 3.2 copy-start.18
  183.2 3.2 copy-start.28
  218.4 6.3 %copy-start.2 = (f32[64,8,8,128]{3,2,1,0:T(8,128)S(1)}, f32[64,8,8,128]{3,2,1,0:T(8,128)}, u32[]{:S(2)}) copy-start(f32[64,8,8,128]{3,2,1,0:T(8,128)} %copy-done.1) | copy-start | bytes 6291460
  218.4 6.3 %copy-start.21 = (f32[8,128,8,64]{1,3,2,0:T(8,128)S(1)}, f32[8,128,8,64]{1,3,2,0:T(8,128)}, u32[]{:S(2)}) copy-start(f32[8,128,8,64]{1,3,2,0:T(8,128)} %copy.159) | copy-start | bytes 6291460
  218.4 6.3 %copy-start.50 = (f32[8]{0:T(128)S(1)}, f32[8]{0:T(128)}, u32[]{:S(2)}) copy-start(f32[8]{0:T(128)} %copy-done.49) | copy-start | bytes 100
  237.7 1.9 copy-start.45
  237.7 1.9 copy-start.52
  253.1 40.8 %copy-start.11 = (bf16[1024,512]{1,0:T(8,128)(2,1)S(1)}, bf16[1024,512]{1,0:T(8,128)(2,1)}, u32[]{:S(2)}) copy-start(bf16[1024,512]{1,0:T(8,128)(2,1)} %param.17) | copy-start | bytes 3145732
  305.4 23.0 %all-to-all-start.5 = ((bf16[16,2,1,32,512]{4,3,1,2,0:T(8,128)(2,1)}), bf16[16,2,1,32,512]{4,3,1,2,0:T(8,128)(2,1)S(1)}, u32[]{:S(2)}, u32[]{:S(2)}) async-start(bf16[16,2,1,32,512]{4,3,1,2,0:T(8,128)(2,1)} %copy.164), calls=%async_computation.6 | async-start | bytes 2097152 | tf_op jit(solution)/shard_map/all_to_all | solution.py:46
  312.1 67.3 %all-gather.6.cloned.1.call-start = ((), (), s32[]{:S(2)}) async-start(), calls=%async_computation.13 | async-start | bytes 5242880 | tf_op jit(solution)/shard_map/all_gather | solution.py:160
  339.0 43.6 %copy-start.37 = (f32[1,2048]{1,0:T(1,128)S(1)}, f32[1,2048]{1,0:T(1,128)}, u32[]{:S(2)}) copy-start(f32[1,2048]{1,0:T(1,128)} %get-tuple-element.155) | copy-start | bytes 24580
  379.4 3.4 copy-start.15
  390.0 1.7 copy-start.17
  390.0 1.7 copy-start.56
  390.1 1.7 copy-start.59
  420.6 16.7 %copy-start.38 = (f32[1,1,256]{2,1,0:T(1,128)S(1)}, f32[1,1,256]{2,1,0:T(1,128)}, u32[]{:S(2)}) copy-start(f32[1,1,256]{2,1,0:T(1,128)} %get-tuple-element.157) | copy-start | bytes 3076
  420.6 16.7 %copy-start.39 = (f32[1,1,256]{2,1,0:T(1,128)S(1)}, f32[1,1,256]{2,1,0:T(1,128)}, u32[]{:S(2)}) copy-start(f32[1,1,256]{2,1,0:T(1,128)} %get-tuple-element.158) | copy-start | bytes 3076
  420.6 16.7 %copy-start.40 = (f32[1,1,256]{2,1,0:T(1,128)S(1)}, f32[1,1,256]{2,1,0:T(1,128)}, u32[]{:S(2)}) copy-start(f32[1,1,256]{2,1,0:T(1,128)} %get-tuple-element.163) | copy-start | bytes 3076
  420.6 16.7 %copy-start.41 = (f32[1,1,256]{2,1,0:T(1,128)S(1)}, f32[1,1,256]{2,1,0:T(1,128)}, u32[]{:S(2)}) copy-start(f32[1,1,256]{2,1,0:T(1,128)} %get-tuple-element.164) | copy-start | bytes 3076
  421.3 14.8 %collective-permute-start.3 = (bf16[3,256]{1,0:T(4,128)(2,1)}, bf16[3,256]{1,0:T(4,128)(2,1)S(1)}, u32[]{:S(2)}, u32[]{:S(2)}) collective-permute-start(bf16[3,256]{1,0:T(4,128)(2,1)} %slice.336), channel_id=1, source_target_pairs={{0,4},{4,8},{8,12},{12,16},{16,20},{20,24},{24,28},{28,32},{32,36}... | collective-permute-start | bytes 4616 | tf_op jit(solution)/shard_map/ppermute | solution.py:33
  425.4 13.5 %collective-permute-start.2 = (bf16[3,512]{1,0:T(4,128)(2,1)S(1)}, bf16[3,512]{1,0:T(4,128)(2,1)S(1)}, u32[]{:S(2)}, u32[]{:S(2)}) collective-permute-start(bf16[3,512]{1,0:T(4,128)(2,1)S(1)} %slice.330), channel_id=1, source_target_pairs={{0,4},{4,8},{8,12},{12,16},{16,20},{20,24},{24,28},{28,32},{32,36}... | collective-permute-start | bytes 9224 | tf_op jit(solution)/shard_map/ppermute | solution.py:33
  428.5 40.3 %all-to-all-start.6 = ((f32[32,1,8]{2,1,0:T(1,128)}), f32[32,1,8]{2,1,0:T(1,128)S(1)}, u32[]{:S(2)}, u32[]{:S(2)}) async-start(f32[32,1,8]{2,1,0:T(1,128)} %broadcast_in_dim.112), calls=%async_computation.7 | async-start | bytes 32768 | tf_op jit(solution)/shard_map/all_to_all | solution.py:23
  447.2 2.0 copy-start.3
  447.2 2.0 copy-start.9
  471.9 7.6 %copy-start.47 = (f32[8]{0:T(128)S(1)}, f32[8]{0:T(128)}, u32[]{:S(2)}) copy-start(f32[8]{0:T(128)} %get-tuple-element.169) | copy-start | bytes 100
  471.9 8.5 %copy-start.25 = (f32[8,8]{1,0:T(8,128)S(1)}, f32[8,8]{1,0:T(8,128)}, u32[]{:S(2)}) copy-start(f32[8,8]{1,0:T(8,128)} %get-tuple-element.141) | copy-start | bytes 772
  471.9 57.8 %all-to-all-start.7 = ((bf16[32,1,8,64,128]{4,3,2,1,0:T(8,128)(2,1)}), bf16[32,1,8,64,128]{4,3,2,1,0:T(8,128)(2,1)}, u32[]{:S(2)}, u32[]{:S(2)}) async-start(bf16[32,1,8,64,128]{4,3,2,1,0:T(8,128)(2,1)} %stack.5), calls=%async_computation.8 | async-start | bytes 8388608 | tf_op jit(solution)/shard_map/all_to_all | solution.py:83
  479.5 125.3 %reduce-scatter.5.cloned.1.call-start = ((), (), s32[]{:S(2)}) async-start(), calls=%async_computation.12 | async-start | bytes 5242880 | tf_op jit(solution)/shard_map/reduce_scatter | solution.py:164
  486.5 4.4 copy-start.35
  486.5 4.7 copy-start.10
  486.5 5.9 copy-start.6
  492.4 3.2 copy-start.19
  492.4 3.2 copy-start.29
  529.7 6.0 copy-start.4
  529.7 6.0 copy-start.20
  529.7 6.0 copy-start.48
  548.7 2.0 copy-start.46
  548.7 1.9 copy-start.51
  559.1 45.7 %copy-start = (bf16[1024,512]{1,0:T(8,128)(2,1)S(1)}, bf16[1024,512]{1,0:T(8,128)(2,1)}, u32[]{:S(2)}) copy-start(bf16[1024,512]{1,0:T(8,128)(2,1)} %gather_fusion.2) | copy-start | bytes 3145732
  (9 other events, 8.4 us)
Sparse Core Ops, SparseCore 0:
  9.0 51.3 all-gather.3
  248.2 45.6 reduce-scatter.2
  333.8 45.5 all-gather.5
  559.3 45.4 reduce-scatter.4
